TPU v7x, 32 devices: a whole 2x2x4 slice. The times are simulated.
32 devices in a mesh: mesh: 8 (over z, core), run: 4 (over y, x).
Axes of the slice: x: 2, y: 2, z: 4, core: 2. Of those that a mesh axis runs over, the one named last changes fastest.
Arguments:
- snapshots: bfloat16 [16384, 2048], P('mesh', 'run'), may hold values from -6 to 6
- block_cols: int32 [256, 16], P('mesh'), may hold values from 0 to 255, as said below
- mass_blocks: bfloat16 [256, 64, 1024], P('mesh'), as said below
Outputs:
- gram: float32 [2048, 2048], P('mesh', 'run')
Inputs may be any that keep to these rules, and one draw needn't show every extreme that they name: `block_cols`: block row b names 16 different block columns, the first of them b itself; all lie from 2 blocks before the first block row of shard b // 32 to 2 blocks after its last. In every shard but the first, its first block row names the block 2 before the shard; in every shard but the last, its last block row names the block 2 after it. `mass_blocks`: entry [b, i, k * 64 + j] is row i, column j of the k-th stored block of block row b, in the order of block_cols.
All inputs are finite; a program needn't handle non-finite values.
Results may differ from a plain program's by a relative error of at most 0.00056.
Values may be sent and summed in bfloat16 or wider, within the bound.
No kernel may reach another device: no remote copies, remote signals or barrier semaphores. Data moves between devices by JAX's collectives and lax.ppermute only.
A program may use at most 128 MiB of HBM per device.

v0:
```python
import jax
import jax.numpy as jnp
from jax import lax
from jax.sharding import PartitionSpec as P

BLK = 64
HB = 2


def extended(block, sides, width):
    for axis, dim in sides:
        count = lax.axis_size(axis)
        forward = [(i, i + 1) for i in range(count - 1)]
        backward = [(target, source) for source, target in forward]
        low = lax.ppermute(
            lax.slice_in_dim(block, block.shape[dim] - width, None, axis=dim), axis, forward
        )
        high = lax.ppermute(lax.slice_in_dim(block, 0, width, axis=dim), axis, backward)
        block = jnp.concatenate([low, block, high], axis=dim)
    return block


def contract_nodes(left_cols, right_cols):
    return lax.dot_general(
        left_cols, right_cols, (((0,), (0,)), ((), ())), preferred_element_type=jnp.float32
    )


def on_device(snapshots, block_cols, mass_blocks):
    node_count = snapshots.shape[0]
    column_count = snapshots.shape[1]
    blocks_here = node_count // BLK
    stored_count = block_cols.shape[1]
    rim_width = HB * BLK
    padded = extended(snapshots, (("mesh", 0),), rim_width)
    shard_index = lax.axis_index("mesh")
    local_cols = block_cols - (shard_index * blocks_here - HB)
    blocked = padded.reshape(blocks_here + 2 * HB, BLK, column_count)
    picked = blocked[local_cols].reshape(blocks_here, stored_count * BLK, column_count)
    weighted = jnp.einsum("bim,bmc->bic", mass_blocks, picked, preferred_element_type=jnp.float32)
    weighted = weighted.astype(jnp.bfloat16).reshape(node_count, column_count)
    gathered = lax.all_gather(snapshots, "run", axis=1, tiled=True)
    return lax.psum_scatter(
        contract_nodes(gathered, weighted), "mesh", scatter_dimension=0, tiled=True
    )


def solution(mesh):
    placed = (P("mesh", "run"), P("mesh", None), P("mesh", None, None))
    return jax.shard_map(
        on_device, mesh=mesh, in_specs=placed, out_specs=P("mesh", "run"), check_vma=False
    )
```

profile of v0, /device:TPU:0, one launch (start us, length us, event | category | flops | bytes accessed | tf_op | source)
XLA Modules:
  0.0 167.7 jit_solution(6542890312637564476)
XLA Ops:
  6.5 0.0 all-gather.2.cloned.1.call-start
  6.5 0.7 all-gather.2.cloned.1.call-update
  7.3 0.0 reduce-scatter.2.cloned.1.call-start
  7.3 1.0 fusion
  8.3 2.4 %collective-permute-start = (bf16[128,512]{1,0:T(8,128)(2,1)S(1)}, bf16[128,512]{1,0:T(8,128)(2,1)S(1)}, u32[]{:S(2)}, u32[]{:S(2)}) collective-permute-start(bf16[128,512]{1,0:T(8,128)(2,1)S(1)} %get-tuple-element.5), channel_id=1, source_target_pairs={{0,4},{4,8},{8,12},{12,16},{16,20},{20,24},{24,28},{1,5},{5,9},{9,... | collective-permute-start | bytes 393224 | tf_op jit(solution)/shard_map/ppermute | solution.py:15
  10.7 1.3 collective-permute-start.1
  12.0 0.7 compare_select_fusion
  12.7 0.1 copy.5
  12.8 0.1 reshape.14
  12.9 0.0 collective-permute-done
  12.9 3.2 %collective-permute-done.1 = bf16[128,512]{1,0:T(8,128)(2,1)S(1)} collective-permute-done((bf16[128,512]{1,0:T(8,128)(2,1)S(1)}, bf16[128,512]{1,0:T(8,128)(2,1)S(1)}, u32[]{:S(2)}, u32[]{:S(2)}) %collective-permute-start.1) | collective-permute-done | bytes 131104 | tf_op jit(solution)/shard_map/ppermute | solution.py:18
  16.1 1.7 %pad_maximum_fusion = bf16[2304,512]{1,0:T(8,128)(2,1)S(1)} fusion(bf16[128,512]{1,0:T(8,128)(2,1)S(1)} %collective-permute-done.1, bf16[2048,512]{1,0:T(8,128)(2,1)} %param.3, bf16[128,512]{1,0:T(8,128)(2,1)S(1)} %collective-permute-done), kind=kLoop, calls=%fused_computation.2 | loop fusion | flops 7077888 | bytes 4718592 | tf_op jit(solution)/shard_map/concatenate | solution.py:19
  17.9 16.1 %gather_fusion = bf16[512,64,512]{2,1,0:T(8,128)(2,1)} fusion(bf16[36,64,512]{2,1,0:T(8,128)(2,1)S(1)} %bitcast.11, s32[1024]{0:T(1024)S(1)} %pad_clamp_fusion), kind=kCustom, calls=%fused_computation | custom fusion | bytes 67110912 | tf_op jit(solution)/shard_map/gather | solution.py:39
  34.0 17.3 %convolution_convert_fusion = bf16[32,512,64]{1,2,0:T(8,128)(2,1)S(1)} fusion(bf16[32,64,1024]{2,1,0:T(8,128)(2,1)} %param.5, bf16[32,1024,512]{2,1,0:T(8,128)(2,1)} %bitcast.12), kind=kOutput, calls=%fused_computation.3 | convolution fusion | flops 2148532224 | bytes 39845888 | tf_op jit(solution)/shard_map/bim,bmc->bic/dot_general | solution.py:40
  51.2 48.0 %all-gather.2.cloned.1.call-done = bf16[2048,2048]{1,0:T(8,128)(2,1)} async-done(((bf16[2048,512]{1,0:T(8,128)(2,1)}), bf16[2048,2048]{1,0:T(8,128)(2,1)}) %all-gather.2.cloned.1.call-update) | async-done | bytes 8388624 | tf_op jit(solution)/shard_map/all_gather | solution.py:42
  99.3 9.4 %convolution_bitcast_fusion = f32[2048,512]{0,1:T(8,128)} fusion(bf16[2048,512]{1,0:T(8,128)(2,1)S(1)} %bitcast.13, bf16[2048,2048]{1,0:T(8,128)(2,1)} %all-gather.2.cloned.1.call-done), kind=kOutput, calls=%fused_computation.1 | convolution fusion | flops 4294967296 | bytes 14680064 | tf_op jit(solution)/shard_map/dot_general | solution.py:24
  108.7 0.0 reduce-scatter.2.cloned.1.call-update
  108.7 50.1 %reduce-scatter.2.cloned.1.call-done = f32[256,512]{0,1:T(8,128)} async-done(((f32[2048,512]{0,1:T(8,128)}), f32[256,512]{0,1:T(8,128)}) %reduce-scatter.2.cloned.1.call-update) | async-done | bytes 524304 | tf_op jit(solution)/shard_map/reduce_scatter | solution.py:43
  158.8 2.0 %copy.6 = f32[256,512]{1,0:T(8,128)} copy(f32[256,512]{0,1:T(8,128)} %reduce-scatter.2.cloned.1.call-done) | data formatting | bytes 1048576 | tf_op jit(solution)/shard_map/reduce_scatter | solution.py:43
  (1 shorter events, 0.0 us)
Async XLA Ops:
  6.5 92.7 %all-gather.2.cloned.1.call-start = ((), (), s32[]{:S(2)}) async-start(), calls=%async_computation.1 | async-start | bytes 10485760 | tf_op jit(solution)/shard_map/all_gather | solution.py:42
  7.3 151.5 %reduce-scatter.2.cloned.1.call-start = ((), (), s32[]{:S(2)}) async-start(), calls=%async_computation.2 | async-start | bytes 4718592 | tf_op jit(solution)/shard_map/reduce_scatter | solution.py:43
  8.3 4.6 %collective-permute-start = (bf16[128,512]{1,0:T(8,128)(2,1)S(1)}, bf16[128,512]{1,0:T(8,128)(2,1)S(1)}, u32[]{:S(2)}, u32[]{:S(2)}) collective-permute-start(bf16[128,512]{1,0:T(8,128)(2,1)S(1)} %get-tuple-element.5), channel_id=1, source_target_pairs={{0,4},{4,8},{8,12},{12,16},{16,20},{20,24},{24,28},{1,5},{5,9},{9,... | collective-permute-start | bytes 393224 | tf_op jit(solution)/shard_map/ppermute | solution.py:15
  10.7 5.4 %collective-permute-start.1 = (bf16[128,512]{1,0:T(8,128)(2,1)S(1)}, bf16[128,512]{1,0:T(8,128)(2,1)S(1)}, u32[]{:S(2)}, u32[]{:S(2)}) collective-permute-start(bf16[128,512]{1,0:T(8,128)(2,1)S(1)} %get-tuple-element.6), channel_id=1, source_target_pairs={{4,0},{8,4},{12,8},{16,12},{20,16},{24,20},{28,24},{5,1},{9,5},{13... | collective-permute-start | bytes 393224 | tf_op jit(solution)/shard_map/ppermute | solution.py:18
Sparse Core Ops, SparseCore 0:
  9.2 90.0 all-gather.1
  108.8 49.8 reduce-scatter.1
where the time goes:
time: 168 us
  waiting for transfers between devices  102 us (61%)
  matrix products  26.7 us (16%)
  local copies, waits for them, and re-layouts  19.3 us (11%)
  between operations  13.4 us (8%)
  starting transfers between devices  3.74 us (2%)
  other arithmetic  2.46 us (1%)
    reduce_scatter x1, waiting for transfers between devices, on_device(): lax.psum_scatter(contract_nodes(gathered, weighted), 'mesh', scatter_dime...  50.1 us
    all_gather x1, waiting for transfers between devices, on_device(): gathered = lax.all_gather(snapshots, 'run', axis=1, tiled=True)  48 us
    dot_general x1, matrix products, on_device(): jnp.einsum('bim,bmc->bic', mass_blocks, picked, preferred_element_type=jn...  17.3 us
    gather x1, local copies, waits for them, and re-layouts, on_device(): blocked[local_cols].reshape(blocks_here, stored_count * BLK, column_count)  16.1 us
    dot_general x1, matrix products, contract_nodes(): lax.dot_general(left_cols, right_cols, (((0,), (0,)), ((), ())), preferre...  9.44 us
  transfers between devices with their start and end apart: 4, of which 3 were waited for; matrix products, arithmetic and copies ran while one was open for 22% of the time, Pallas kernels for 0%

commit v1 on v0

--- a/solution.py
+++ b/solution.py
@@ -39,7 +39,9 @@
     picked = blocked[local_cols].reshape(blocks_here, stored_count * BLK, column_count)
     weighted = jnp.einsum("bim,bmc->bic", mass_blocks, picked, preferred_element_type=jnp.float32)
     weighted = weighted.astype(jnp.bfloat16).reshape(node_count, column_count)
-    gathered = lax.all_gather(snapshots, "run", axis=1, tiled=True)
+    gathered = jnp.concatenate(
+        lax.all_to_all(jnp.stack([snapshots] * lax.axis_size("run")), "run", 0, 0), axis=1
+    )
     return lax.psum_scatter(
         contract_nodes(gathered, weighted), "mesh", scatter_dimension=0, tiled=True
     )

time: 168 us -> 183 us (1.089)
  local copies, waits for them, and re-layouts: 19.3 us -> 26.5 us
  starting transfers between devices: 3.74 us -> 9.51 us
  waiting for transfers between devices: 102 us -> 104 us
    all_to_all x0 -> x1, waiting for transfers between devices: none -> 49.9 us  [on_device(): lax.all_to_all(jnp.stack([snapshots] * lax.axis_size('run')), 'run', 0, 0)]
    all_gather x1 -> x0, waiting for transfers between devices: 48 us -> none  [on_device(): gathered = lax.all_gather(snapshots, 'run', axis=1, tiled=True)]
    all_to_all x0 -> x1, starting transfers between devices: none -> 5.77 us  [on_device(): lax.all_to_all(jnp.stack([snapshots] * lax.axis_size('run')), 'run', 0, 0)]
    another operation x0 -> x1, local copies, waits for them, and re-layouts: none -> 4.26 us  [on_device(): jnp.stack([snapshots] * lax.axis_size('run'))]
    unnamed x0 -> x3, local copies, waits for them, and re-layouts: none -> 2.93 us
  transfers between devices with their start and end apart: 4 -> 4, of which waited for: 3 -> 3; matrix products, arithmetic and copies ran while one was open for 22% -> 20% of each run, Pallas kernels for 0% -> 0%
where the time goes in v1:
time: 183 us; the launch traced here: 182 us
  waiting for transfers between devices  104 us (57%)
  matrix products  26.9 us (15%)
  local copies, waits for them, and re-layouts  26.5 us (14%)
  between operations  13.5 us (7%)
  starting transfers between devices  9.51 us (5%)
    reduce_scatter x1, waiting for transfers between devices, on_device(): lax.psum_scatter(contract_nodes(gathered, weighted), 'mesh', scatter_dime...  50.6 us
    all_to_all x1, waiting for transfers between devices, on_device(): lax.all_to_all(jnp.stack([snapshots] * lax.axis_size('run')), 'run', 0, 0)  49.9 us
    dot_general x1, matrix products, on_device(): jnp.einsum('bim,bmc->bic', mass_blocks, picked, preferred_element_type=jn...  17.3 us
    gather x1, local copies, waits for them, and re-layouts, on_device(): blocked[local_cols].reshape(blocks_here, stored_count * BLK, column_count)  16.1 us
    dot_general x1, matrix products, contract_nodes(): lax.dot_general(left_cols, right_cols, (((0,), (0,)), ((), ())), preferre...  9.62 us
    all_to_all x1, starting transfers between devices, on_device(): lax.all_to_all(jnp.stack([snapshots] * lax.axis_size('run')), 'run', 0, 0)  5.77 us
    another operation x1, local copies, waits for them, and re-layouts, on_device(): jnp.stack([snapshots] * lax.axis_size('run'))  4.26 us
    ppermute x1, waiting for transfers between devices, extended(): lax.ppermute(lax.slice_in_dim(block, 0, width, axis=dim), axis, backward)  3.91 us
  transfers between devices with their start and end apart: 4, of which 3 were waited for; matrix products, arithmetic and copies ran while one was open for 20% of the time, Pallas kernels for 0%

profile of v1, /device:TPU:0, one launch (start us, length us, event | category | flops | bytes accessed | tf_op | source)
XLA Modules:
  0.0 182.5 jit_solution(2643853402996531500)
XLA Ops:
  6.5 2.9 %copy.6 = bf16[2048,512]{0,1:T(8,128)(2,1)S(1)} copy(bf16[2048,512]{1,0:T(8,128)(2,1)} %param.3) | data formatting | bytes 4194304 | tf_op args[0]
  9.5 4.3 %stack.2 = bf16[4,2048,512]{1,2,0:T(8,128)(2,1)} broadcast(bf16[2048,512]{0,1:T(8,128)(2,1)S(1)} %copy.6), dimensions={1,2} | broadcast | bytes 10485760 | tf_op jit(solution)/shard_map/stack | solution.py:43
  13.7 0.0 copy-start
  13.7 5.8 %all-to-all-start = ((bf16[4,2048,512]{1,2,0:T(8,128)(2,1)}), bf16[4,2048,512]{1,2,0:T(8,128)(2,1)}, u32[]{:S(2)}, u32[]{:S(2)}) async-start(bf16[4,2048,512]{1,2,0:T(8,128)(2,1)} %stack.2), calls=%async_computation | async-start | bytes 16777216 | tf_op jit(solution)/shard_map/all_to_all | solution.py:43
  19.5 0.0 reduce-scatter.2.cloned.1.call-start
  19.6 1.0 fusion
  20.6 2.4 %collective-permute-start = (bf16[128,512]{1,0:T(8,128)(2,1)S(1)}, bf16[128,512]{1,0:T(8,128)(2,1)S(1)}, u32[]{:S(2)}, u32[]{:S(2)}) collective-permute-start(bf16[128,512]{1,0:T(8,128)(2,1)S(1)} %get-tuple-element.5), channel_id=1, source_target_pairs={{0,4},{4,8},{8,12},{12,16},{16,20},{20,24},{24,28},{1,5},{5,9},{9,... | collective-permute-start | bytes 393224 | tf_op jit(solution)/shard_map/ppermute | solution.py:15
  23.0 1.3 collective-permute-start.1
  24.3 0.0 copy-done
  24.3 0.1 copy.5
  24.4 0.1 reshape.24
  24.5 0.0 collective-permute-done
  24.5 3.9 %collective-permute-done.1 = bf16[128,512]{1,0:T(8,128)(2,1)S(1)} collective-permute-done((bf16[128,512]{1,0:T(8,128)(2,1)S(1)}, bf16[128,512]{1,0:T(8,128)(2,1)S(1)}, u32[]{:S(2)}, u32[]{:S(2)}) %collective-permute-start.1) | collective-permute-done | bytes 131104 | tf_op jit(solution)/shard_map/ppermute | solution.py:18
  28.4 1.7 pad_maximum_fusion
  30.1 16.1 %gather_fusion = bf16[512,64,512]{2,1,0:T(8,128)(2,1)} fusion(bf16[36,64,512]{2,1,0:T(8,128)(2,1)S(1)} %bitcast.14, s32[1024]{0:T(1024)S(1)} %pad_clamp_fusion), kind=kCustom, calls=%fused_computation | custom fusion | bytes 67110912 | tf_op jit(solution)/shard_map/gather | solution.py:39
  46.2 17.3 %convolution_convert_fusion = bf16[32,512,64]{1,2,0:T(8,128)(2,1)S(1)} fusion(bf16[32,64,1024]{2,1,0:T(8,128)(2,1)} %param.5, bf16[32,1024,512]{2,1,0:T(8,128)(2,1)} %bitcast.15), kind=kOutput, calls=%fused_computation.3 | convolution fusion | flops 2148532224 | bytes 39845888 | tf_op jit(solution)/shard_map/bim,bmc->bic/dot_general | solution.py:40
  63.5 49.9 %all-to-all-done = bf16[4,2048,512]{1,2,0:T(8,128)(2,1)} async-done(((bf16[4,2048,512]{1,2,0:T(8,128)(2,1)}), bf16[4,2048,512]{1,2,0:T(8,128)(2,1)}, u32[]{:S(2)}, u32[]{:S(2)}) %all-to-all-start) | async-done | bytes 8388640 | tf_op jit(solution)/shard_map/all_to_all | solution.py:43
  113.4 9.6 %convolution_bitcast_fusion = f32[2048,512]{0,1:T(8,128)} fusion(bf16[2048,512]{1,0:T(8,128)(2,1)S(1)} %bitcast.16, bf16[2048,2048]{0,1:T(8,128)(2,1)} %bitcast.5), kind=kOutput, calls=%fused_computation.1 | convolution fusion | flops 4294967296 | bytes 14680064 | tf_op jit(solution)/shard_map/dot_general | solution.py:24
  123.0 0.0 reduce-scatter.2.cloned.1.call-update
  123.0 50.6 %reduce-scatter.2.cloned.1.call-done = f32[256,512]{0,1:T(8,128)} async-done(((f32[2048,512]{0,1:T(8,128)}), f32[256,512]{0,1:T(8,128)}) %reduce-scatter.2.cloned.1.call-update) | async-done | bytes 524304 | tf_op jit(solution)/shard_map/reduce_scatter | solution.py:45
  173.6 2.0 %copy.7 = f32[256,512]{1,0:T(8,128)} copy(f32[256,512]{0,1:T(8,128)} %reduce-scatter.2.cloned.1.call-done) | data formatting | bytes 1048576 | tf_op jit(solution)/shard_map/reduce_scatter | solution.py:45
  (2 shorter events, 0.0 us)
Async XLA Ops:
  13.7 10.5 %copy-start = (s32[32,16]{0,1:T(8,128)S(1)}, s32[32,16]{0,1:T(8,128)}, u32[]{:S(2)}) copy-start(s32[32,16]{0,1:T(8,128)} %param.4) | copy-start | bytes 6148
  13.7 99.7 %all-to-all-start = ((bf16[4,2048,512]{1,2,0:T(8,128)(2,1)}), bf16[4,2048,512]{1,2,0:T(8,128)(2,1)}, u32[]{:S(2)}, u32[]{:S(2)}) async-start(bf16[4,2048,512]{1,2,0:T(8,128)(2,1)} %stack.2), calls=%async_computation | async-start | bytes 16777216 | tf_op jit(solution)/shard_map/all_to_all | solution.py:43
  19.5 154.1 %reduce-scatter.2.cloned.1.call-start = ((), (), s32[]{:S(2)}) async-start(), calls=%async_computation.2 | async-start | bytes 4718592 | tf_op jit(solution)/shard_map/reduce_scatter | solution.py:45
  20.6 3.9 %collective-permute-start = (bf16[128,512]{1,0:T(8,128)(2,1)S(1)}, bf16[128,512]{1,0:T(8,128)(2,1)S(1)}, u32[]{:S(2)}, u32[]{:S(2)}) collective-permute-start(bf16[128,512]{1,0:T(8,128)(2,1)S(1)} %get-tuple-element.5), channel_id=1, source_target_pairs={{0,4},{4,8},{8,12},{12,16},{16,20},{20,24},{24,28},{1,5},{5,9},{9,... | collective-permute-start | bytes 393224 | tf_op jit(solution)/shard_map/ppermute | solution.py:15
  23.0 5.4 %collective-permute-start.1 = (bf16[128,512]{1,0:T(8,128)(2,1)S(1)}, bf16[128,512]{1,0:T(8,128)(2,1)S(1)}, u32[]{:S(2)}, u32[]{:S(2)}) collective-permute-start(bf16[128,512]{1,0:T(8,128)(2,1)S(1)} %get-tuple-element.6), channel_id=1, source_target_pairs={{4,0},{8,4},{12,8},{16,12},{20,16},{24,20},{28,24},{5,1},{9,5},{13... | collective-permute-start | bytes 393224 | tf_op jit(solution)/shard_map/ppermute | solution.py:18
Sparse Core Ops, SparseCore 0:
  123.2 50.3 reduce-scatter.1
